TPU v7x, 32 devices: a whole 2x2x4 slice. The times are simulated.
32 devices in a mesh: gx: 2 (over z_hi), gy: 2 (over z_lo), gz: 8 (over y, x, core).
Axes of the slice: x: 2, y: 2, z: 4 (z_hi: 2, z_lo: 2; z = z_hi * 2 + z_lo), core: 2. Of those that a mesh axis runs over, the one named last changes fastest.
Arguments:
- amplitudes: float32 [2, 8388608], P(None, ('gx', 'gy', 'gz')), may hold values from -6 to 6
- gates: float32 [6, 2, 128, 128], replicated, may hold values from -0.375 to 0.375
- gate_wires: int32 [6, 7], replicated, may hold values from 0 to 6, each once within a row
Outputs:
- evolved: float32 [2, 8388608], P(None, ('gx', 'gy', 'gz'))
Inputs may be any that keep to these rules, and one draw needn't show every extreme that they name: Each row of gate_wires is an ordering of the numbers below 7.
All inputs are finite; a program needn't handle non-finite values.
Results may differ from a plain program's by a relative error of at most 0.00007.
Values sent between devices are 32-bit elements; how exact they have to be, the bound alone decides.
No kernel may reach another device: no remote copies, remote signals or barrier semaphores. Data moves between devices by JAX's collectives and lax.ppermute only.
A program may use at most 64 MiB of HBM per device.

v0:
```python
import functools

import jax
import jax.numpy as jnp
from jax import lax
from jax.experimental import pallas as pl
from jax.experimental.pallas import tpu as pltpu
from jax.sharding import PartitionSpec as P

F32 = jnp.float32
BF16 = jnp.bfloat16
VMEM = pl.BlockSpec(memory_space=pltpu.VMEM)
SMEM = pl.BlockSpec(memory_space=pltpu.SMEM)


def bits_of(size):
    count = size.bit_length() - 1
    assert size == 1 << count
    return count


def halves(value):
    high = value.astype(BF16)
    return high, (value - high.astype(F32)).astype(BF16)


def dot(a, b):
    return jnp.dot(a, b, preferred_element_type=F32)


def product(left, right):
    return dot(left[0], right[0]) + (dot(left[0], right[1]) + dot(left[1], right[0]))


def complex_form(real, imag):
    return jnp.concatenate(
        [jnp.concatenate([real, -imag], axis=1), jnp.concatenate([imag, real], axis=1)], axis=0
    )


def row_form(real, imag):
    return jnp.concatenate(
        [jnp.concatenate([real, imag], axis=1), jnp.concatenate([-imag, real], axis=1)], axis=0
    )


def matrices_kernel(wires, flips, gates, lane_out, *left_outs):
    order = gates.shape[-1]
    width = wires.shape[1]
    rows = lax.broadcasted_iota(jnp.int32, (order, order), 0)
    columns = lax.broadcasted_iota(jnp.int32, (order, order), 1)

    def picker(g, flip):
        index = jnp.bitwise_xor(rows, flip)
        mapped = jnp.zeros_like(index)
        for j in range(width):
            bit = jnp.bitwise_and(jnp.right_shift(index, j), 1)
            mapped = mapped + jnp.left_shift(bit, wires[g, j])
        return jnp.where(mapped == columns, 1.0, 0.0).astype(BF16)

    def window(g, transposed):
        row_pick = picker(g, flips[g, 0])
        column_pick = picker(g, flips[g, 1])
        parts = []
        for c in range(2):
            pair = []
            for half in halves(gates[g, c]):
                first = dot(row_pick, half).astype(BF16)
                a, b = (column_pick, first) if transposed else (first, column_pick)
                pair.append(
                    lax.dot_general(a, b, (((1,), (1,)), ((), ())), preferred_element_type=F32)
                )
            parts.append(pair)
        return parts

    first, last = window(0, True), window(4, True)
    a = [jnp.concatenate([first[0][h], first[1][h]], axis=1).astype(BF16) for h in range(2)]
    b = [row_form(last[0][h], last[1][h]).astype(BF16) for h in range(2)]
    both = product(a, b)
    lane = halves(row_form(both[:, :order], both[:, order:]))
    lane_out[0] = lane[0]
    lane_out[1] = lane[1]
    for out, g in zip(left_outs, (1, 2, 3, 5)):
        parts = window(g, False)
        for h in range(2):
            out[h] = complex_form(parts[0][h], parts[1][h]).astype(BF16)


def matrices(gates, wires, flips):
    order = gates.shape[-1]
    shape = jax.ShapeDtypeStruct((2, 2 * order, 2 * order), BF16)
    return pl.pallas_call(
        matrices_kernel,
        out_shape=[shape] * 5,
        in_specs=[SMEM, SMEM, VMEM],
        out_specs=[VMEM] * 5,
        name="matrices",
    )(wires, flips, gates)


def runs(slots):
    merged = []
    for at, (operand, index) in enumerate(slots):
        if merged and merged[-1][0] == operand and merged[-1][1] + merged[-1][3] == index:
            merged[-1][3] += 1
        else:
            merged.append([operand, index, at, 1])
    return merged


def load_top(refs, slots, order, chunk, m, part):
    height = order // len(slots)
    step = 2 * chunk
    pieces = [
        refs[o][pl.ds(i * height * step + 2 * m + part, n * height, stride=step), :]
        for o, i, _, n in runs(slots)
    ]
    return pieces[0] if len(pieces) == 1 else jnp.concatenate(pieces, axis=0)


def store_top(refs, slots, order, chunk, m, part, value):
    height = order // len(slots)
    step = 2 * chunk
    for o, i, at, n in runs(slots):
        refs[o][pl.ds(i * height * step + 2 * m + part, n * height, stride=step), :] = value[
            at * height : (at + n) * height
        ]


def left(matrix, loads):
    columns = jnp.concatenate([jnp.concatenate(pair, axis=0) for pair in loads], axis=1)
    out = product((matrix[0], matrix[1]), halves(columns))
    order = matrix.shape[-1] // 2
    return [
        (out[:order, k * order : (k + 1) * order], out[order:, k * order : (k + 1) * order])
        for k in range(len(loads))
    ]


def top_gate(matrix, lane, order, chunk, sources, in_slots, targets, out_slots):
    per = min(2, chunk)

    def body(i, carry):
        ms = [per * i + k for k in range(per)]
        loads = [
            tuple(load_top(sources, in_slots, order, chunk, m, part) for part in range(2))
            for m in ms
        ]
        done = left(matrix, loads)
        if lane is not None:
            rows = jnp.concatenate([jnp.concatenate(pair, axis=1) for pair in done], axis=0)
            rows = product(halves(rows), (lane[0], lane[1]))
            done = [
                (rows[k * order : (k + 1) * order, :order], rows[k * order : (k + 1) * order, order:])
                for k in range(per)
            ]
        for m, pair in zip(ms, done):
            for part in range(2):
                store_top(targets, out_slots, order, chunk, m, part, pair[part])
        return carry

    lax.fori_loop(0, chunk // per, body, 0)


def inner_gate(matrix, order, middle, sources, slots, target):
    span = 2 * order
    blocks = order * middle // order
    per_slot = blocks // len(slots)
    for o, i, at, n in runs(slots):
        first, count = i * per_slot, n * per_slot
        base = at * per_slot

        def body(k, carry, o=o, first=first, base=base):
            loads = []
            for q in range(2):
                start = pl.multiple_of((first + 2 * k + q) * span, span)
                loads.append(
                    tuple(sources[o][pl.ds(start + part, order, stride=2), :] for part in range(2))
                )
            for q, pair in enumerate(left(matrix, loads)):
                start = pl.multiple_of((base + 2 * k + q) * span, span)
                for part in range(2):
                    target[pl.ds(start + part, order, stride=2), :] = pair[part]
            return carry

        lax.fori_loop(0, count // 2, body, 0)


def first_kernel(order, chunk, in_slots, out_slots, n_in, matrix, lane, *refs):
    top_gate(matrix, lane, order, chunk, refs[:n_in], in_slots, refs[n_in:], out_slots)


def middle_kernel(order, middle, in_slots, out_slots, n_in, inner, matrix, *refs):
    sources, targets, scratch = refs[:n_in], refs[n_in:-1], refs[-1]
    inner_gate(inner, order, middle, sources, in_slots, scratch)
    top_gate(matrix, None, order, middle, [scratch], [(0, 0)], targets, out_slots)


def last_kernel(order, chunk, in_slots, out_slots, n_in, matrix, *refs):
    top_gate(matrix, None, order, chunk, refs[:n_in], in_slots, refs[n_in:], out_slots)


def call(kernel, name, mats, sources, out_rows, lanes, scratch=()):
    return pl.pallas_call(
        kernel,
        out_shape=[jax.ShapeDtypeStruct((rows, lanes), F32) for rows in out_rows],
        in_specs=[VMEM] * (len(mats) + len(sources)),
        out_specs=[VMEM] * len(out_rows),
        scratch_shapes=list(scratch),
        name=name,
    )(*mats, *sources)


def swap(slots, arrays, height, axis, bit, index_bit):
    size = lax.axis_size(axis)
    pairs = [(i, i ^ (1 << bit)) for i in range(size)]
    leaving = [s for s in range(len(slots)) if s >> index_bit & 1]
    parts = [
        arrays[o][i * height : (i + n) * height] for o, i, _, n in runs([slots[s] for s in leaving])
    ]
    send = parts[0] if len(parts) == 1 else jnp.concatenate(parts, axis=0)
    got = lax.ppermute(send, axis, pairs)
    slots, arrays = list(slots), list(arrays) + [got]
    for at, s in enumerate(leaving):
        slots[s] = (len(arrays) - 1, at)
    return slots, arrays


def shards(amplitudes, gates, gate_wires):
    count = amplitudes.shape[1]
    order = gates.shape[-1]
    middle = count // (order * order)
    rows = 2 * count // order
    nx = bits_of(lax.axis_size("gx"))
    top = bits_of(order)
    group = lax.axis_size("gy") * lax.axis_size("gz")
    depth = lax.axis_size("gz")

    flip_x = jnp.left_shift(lax.axis_index("gx"), top - nx)
    zero = jnp.zeros_like(flip_x)
    flips = jnp.stack([zero, zero, flip_x, zero, zero, zero, zero, flip_x, zero, zero, zero, zero])
    lane, m1, m2, m3, m5 = matrices(gates, gate_wires, flips.reshape(6, 2))

    state = amplitudes.reshape(2, count // order, order).transpose(1, 0, 2).reshape(group, rows // group, order)
    state = lax.all_to_all(state, ("gy", "gz"), split_axis=0, concat_axis=0, tiled=True).reshape(rows, order)

    across = 1 << nx
    half = across // 2
    slots = [(s // half, s % half) for s in range(across)]
    arrays = call(
        functools.partial(first_kernel, order, middle, [(0, 0)], slots, 1),
        "first", (m1, lane), [state], [rows // 2] * 2, order,
    )
    for bit in reversed(range(nx)):
        slots, arrays = swap(slots, arrays, rows // across, "gx", bit, bit)
    used = sorted({s[0] for s in slots})
    slots = [(used.index(o), i) for o, i in slots]
    state = call(
        functools.partial(middle_kernel, order, middle, slots, [(0, 0)], len(used)),
        "middle", (m2, m3), [arrays[o] for o in used], [rows], order,
        [pltpu.VMEM((rows, order), F32)],
    )[0]
    state = state.reshape(depth, rows // depth, order)
    state = lax.all_to_all(state, "gz", split_axis=0, concat_axis=0, tiled=True).reshape(rows, order)
    state = call(
        functools.partial(last_kernel, order, middle, [(0, 0)], [(0, 0)], 1),
        "last", (m5,), [state], [rows], order,
    )[0]
    return state.reshape(count // order, 2, order).transpose(1, 0, 2).reshape(2, count)


def solution(mesh):
    in_specs = (P(None, ("gx", "gy", "gz")), P(), P())
    out_specs = P(None, ("gx", "gy", "gz"))
    return jax.shard_map(shards, mesh=mesh, in_specs=in_specs, out_specs=out_specs, check_vma=False)
```

profile of v0, /device:TPU:0, one launch (start us, length us, event | category | flops | bytes accessed | tf_op | source)
XLA Modules:
  0.0 154.2 jit_solution(13339380319094374531)
XLA Ops:
  0.0 1.7 %copy.10 = f32[1,2,2048,128]{3,2,1,0:T(8,128)S(1)} copy(f32[1,2,2048,128]{3,1,2,0:T(2,128)} %bitcast.22) | data formatting | bytes 4194304
  1.7 8.6 %copy.6 = f32[2048,2,128]{2,1,0:T(2,128)} copy(f32[2048,2,128]{2,0,1:T(8,128)S(1)} %bitcast.21) | data formatting | bytes 4194304 | tf_op jit(solution)/shard_map/transpose | solution.py:244
  10.3 6.3 %all-to-all-start = ((f32[16,256,128]{2,1,0:T(8,128)}), f32[16,256,128]{2,1,0:T(8,128)S(1)}, u32[]{:S(2)}, u32[]{:S(2)}) async-start(f32[16,256,128]{2,1,0:T(8,128)} %bitcast.18), calls=%async_computation | async-start | bytes 4194304 | tf_op jit(solution)/shard_map/all_to_all | solution.py:245
  16.6 0.1 stack.8
  16.7 0.7 reshape.24.flips
  17.4 3.9 %matrices.1 = (bf16[2,256,256]{2,1,0:T(8,128)(2,1)}, bf16[2,256,256]{2,1,0:T(8,128)(2,1)}, bf16[2,256,256]{2,1,0:T(8,128)(2,1)}, bf16[2,256,256]{2,1,0:T(8,128)(2,1)}, bf16[2,256,256]{2,1,0:T(8,128)(2,1)}) custom-call(s32[6,7]{1,0:T(8,128)} %wires.1, s32[6,2]{1,0:T(8,128)} %reshape.24.flips, f32[6,2,128,128]{3,2,1,0:T(8,128)} %gates.1), custom_call_target="tpu_custom_call" | custom-call | tf_op jit(solution)/shard_map/matrices/pallas_call | solution.py:92
  21.3 24.3 %all-to-all-done = f32[16,256,128]{2,1,0:T(8,128)S(1)} async-done(((f32[16,256,128]{2,1,0:T(8,128)}), f32[16,256,128]{2,1,0:T(8,128)S(1)}, u32[]{:S(2)}, u32[]{:S(2)}) %all-to-all-start) | async-done | bytes 2097184 | tf_op jit(solution)/shard_map/all_to_all | solution.py:245
  45.7 0.0 copy-start
  45.7 1.3 copy-done
  47.0 10.2 %first.1 = (f32[2048,128]{1,0:T(8,128)}, f32[2048,128]{1,0:T(8,128)}) custom-call(bf16[2,256,256]{2,1,0:T(8,128)(2,1)} %get-tuple-element.15.matrix, bf16[2,256,256]{2,1,0:T(8,128)(2,1)} %get-tuple-element.16.lane, f32[4096,128]{1,0:T(8,128)} %bitcast.17), custom_call_target="tpu_custom_call" | custom-call | tf_op jit(solution)/shard_map/first/pallas_call | solution.py:204
  57.2 2.6 %collective-permute-start = (f32[2048,128]{1,0:T(8,128)}, f32[2048,128]{1,0:T(8,128)S(1)}, u32[]{:S(2)}, u32[]{:S(2)}) collective-permute-start(f32[2048,128]{1,0:T(8,128)} %get-tuple-element.18), channel_id=1, source_target_pairs={{0,16},{16,0},{1,17},{17,1},{2,18},{18,2},{3,19},{19,3},{4,20},{20... | collective-permute-start | bytes 3145736 | tf_op jit(solution)/shard_map/ppermute | solution.py:222
  59.7 45.6 %collective-permute-done.refs_1_ = f32[2048,128]{1,0:T(8,128)S(1)} collective-permute-done((f32[2048,128]{1,0:T(8,128)}, f32[2048,128]{1,0:T(8,128)S(1)}, u32[]{:S(2)}, u32[]{:S(2)}) %collective-permute-start) | collective-permute-done | bytes 1048608 | tf_op jit(solution)/shard_map/ppermute | solution.py:222
  105.3 0.0 copy-start.1
  105.3 1.0 copy-done.1
  106.4 9.2 %middle.1 = f32[4096,128]{1,0:T(8,128)} custom-call(bf16[2,256,256]{2,1,0:T(8,128)(2,1)} %get-tuple-element.13.inner, bf16[2,256,256]{2,1,0:T(8,128)(2,1)} %get-tuple-element.14.matrix, f32[2048,128]{1,0:T(8,128)} %get-tuple-element.17.refs_0_, f32[2048,128]{1,0:T(8,128)} %copy-done.1), custom_call_target="tpu_custom_call" | custom-call | tf_op jit(solution)/shard_map/middle/pallas_call | solution.py:204
  115.6 31.5 %all_to_all.10 = f32[8,512,128]{2,1,0:T(8,128)} all-to-all(f32[8,512,128]{2,1,0:T(8,128)} %bitcast.19), channel_id=1, replica_groups=mesh['gx'=2,'gy'=2,'gz'=8] {'gz'}, dimensions={0} | all-to-all | bytes 4194304 | tf_op jit(solution)/shard_map/all_to_all | solution.py:264
  147.2 7.1 %last.1 = f32[4096,128]{1,0:T(8,128)} custom-call(bf16[2,256,256]{2,1,0:T(8,128)(2,1)} %get-tuple-element.12.matrix, f32[4096,128]{1,0:T(8,128)} %bitcast.20), custom_call_target="tpu_custom_call" | custom-call | tf_op jit(solution)/shard_map/last/pallas_call | solution.py:204
  (2 shorter events, 0.0 us)
Async XLA Ops:
  10.3 35.4 %all-to-all-start = ((f32[16,256,128]{2,1,0:T(8,128)}), f32[16,256,128]{2,1,0:T(8,128)S(1)}, u32[]{:S(2)}, u32[]{:S(2)}) async-start(f32[16,256,128]{2,1,0:T(8,128)} %bitcast.18), calls=%async_computation | async-start | bytes 4194304 | tf_op jit(solution)/shard_map/all_to_all | solution.py:245
  45.7 1.3 copy-start
  57.2 48.2 %collective-permute-start = (f32[2048,128]{1,0:T(8,128)}, f32[2048,128]{1,0:T(8,128)S(1)}, u32[]{:S(2)}, u32[]{:S(2)}) collective-permute-start(f32[2048,128]{1,0:T(8,128)} %get-tuple-element.18), channel_id=1, source_target_pairs={{0,16},{16,0},{1,17},{17,1},{2,18},{18,2},{3,19},{19,3},{4,20},{20... | collective-permute-start | bytes 3145736 | tf_op jit(solution)/shard_map/ppermute | solution.py:222
  105.3 1.0 copy-start.1
where the time goes:
time: 155 us; the launch traced here: 154 us
  waiting for transfers between devices  69.9 us (45%)
  blocking collectives  31.5 us (20%)
  Pallas kernels  30.4 us (20%)
  local copies, waits for them, and re-layouts  13.4 us (9%)
  starting transfers between devices  8.9 us (6%)
    ppermute x1, waiting for transfers between devices, swap(): got = lax.ppermute(send, axis, pairs)  45.6 us
    all_to_all x1, blocking collectives, shards(): lax.all_to_all(state, 'gz', split_axis=0, concat_axis=0, tiled=True)  31.5 us
    pallas_call x3, Pallas kernels, call(): pl.pallas_call(kernel, out_shape=[jax.ShapeDtypeStruct((rows, lanes), F32...  26.5 us
    all_to_all x1, waiting for transfers between devices, shards(): lax.all_to_all(state, ('gy', 'gz'), split_axis=0, concat_axis=0, tiled=True)  24.3 us
    transpose x1, local copies, waits for them, and re-layouts, shards(): amplitudes.reshape(2, count // order, order).transpose(1, 0, 2)  8.55 us
    all_to_all x1, starting transfers between devices, shards(): lax.all_to_all(state, ('gy', 'gz'), split_axis=0, concat_axis=0, tiled=True)  6.32 us
    unnamed x5, local copies, waits for them, and re-layouts  4.08 us
    pallas_call x1, Pallas kernels, matrices(): pl.pallas_call(matrices_kernel, out_shape=[shape] * 5, in_specs=[SMEM, SM...  3.94 us
  transfers between devices with their start and end apart: 2, of which 2 were waited for; matrix products, arithmetic and copies ran while one was open for 0% of the time, Pallas kernels for 3%

commit v1 on v0

v1 whole, which is shorter than its diff:
```python
import functools

import jax
import jax.numpy as jnp
from jax import lax
from jax.experimental import pallas as pl
from jax.experimental.pallas import tpu as pltpu
from jax.experimental.layout import Layout, with_layout_constraint
from jax.sharding import PartitionSpec as P

F32 = jnp.float32
BF16 = jnp.bfloat16
VMEM = pl.BlockSpec(memory_space=pltpu.VMEM)
ANY = pl.BlockSpec(memory_space=pl.ANY)
LIMIT = pltpu.CompilerParams(vmem_limit_bytes=20 << 20)
SMEM = pl.BlockSpec(memory_space=pltpu.SMEM)


def bits_of(size):
    count = size.bit_length() - 1
    assert size == 1 << count
    return count


def in_vmem(shape):
    return pltpu.VMEM(shape.shape, shape.dtype)


def keep(value):
    return pltpu.with_memory_space_constraint(value, pltpu.VMEM)


def halves(value):
    high = value.astype(BF16)
    return high, (value - high.astype(F32)).astype(BF16)


def dot(a, b):
    return jnp.dot(a, b, preferred_element_type=F32)


def product(left, right):
    return dot(left[0], right[0]) + (dot(left[0], right[1]) + dot(left[1], right[0]))


def complex_form(real, imag):
    return jnp.concatenate(
        [jnp.concatenate([real, -imag], axis=1), jnp.concatenate([imag, real], axis=1)], axis=0
    )


def row_form(real, imag):
    return jnp.concatenate(
        [jnp.concatenate([real, imag], axis=1), jnp.concatenate([-imag, real], axis=1)], axis=0
    )


def matrices_kernel(middle, chunks, wires, flips, gates, lane_out, *left_outs):
    order = gates.shape[-1]
    width = wires.shape[1]
    rows = lax.broadcasted_iota(jnp.int32, (order, order), 0)
    columns = lax.broadcasted_iota(jnp.int32, (order, order), 1)

    def picker(g, flip):
        index = jnp.bitwise_xor(rows, flip)
        if g == 2:
            rest = bits_of(middle // chunks)
            low = bits_of(order // middle)
            index = (
                jnp.left_shift(jnp.bitwise_and(jnp.right_shift(rows, rest), (1 << low) - 1), bits_of(middle))
                + jnp.left_shift(jnp.right_shift(rows, rest + low), rest)
                + jnp.bitwise_and(rows, (1 << rest) - 1)
            )
        mapped = jnp.zeros_like(index)
        for j in range(width):
            bit = jnp.bitwise_and(jnp.right_shift(index, j), 1)
            mapped = mapped + jnp.left_shift(bit, wires[g, j])
        return jnp.where(mapped == columns, 1.0, 0.0).astype(BF16)

    def window(g, transposed):
        row_pick = picker(g, flips[g, 0])
        column_pick = picker(g, flips[g, 1])
        parts = []
        for c in range(2):
            pair = []
            for half in halves(gates[g, c]):
                first = dot(row_pick, half).astype(BF16)
                a, b = (column_pick, first) if transposed else (first, column_pick)
                pair.append(
                    lax.dot_general(a, b, (((1,), (1,)), ((), ())), preferred_element_type=F32)
                )
            parts.append(pair)
        return parts

    first, last = window(0, True), window(4, True)
    a = [jnp.concatenate([first[0][h], first[1][h]], axis=1).astype(BF16) for h in range(2)]
    b = [row_form(last[0][h], last[1][h]).astype(BF16) for h in range(2)]
    both = product(a, b)
    lane = halves(row_form(both[:, :order], both[:, order:]))
    lane_out[0] = lane[0]
    lane_out[1] = lane[1]
    for out, g in zip(left_outs, (1, 2, 3, 5)):
        parts = window(g, False)
        for h in range(2):
            out[h] = complex_form(parts[0][h], parts[1][h]).astype(BF16)


def matrices(gates, wires, flips, middle, chunks):
    order = gates.shape[-1]
    shape = jax.ShapeDtypeStruct((2, 2 * order, 2 * order), BF16)
    return pl.pallas_call(
        functools.partial(matrices_kernel, middle, chunks),
        out_shape=[in_vmem(shape)] * 5,
        in_specs=[SMEM, SMEM, VMEM],
        out_specs=[VMEM] * 5,
        compiler_params=LIMIT,
        name="matrices",
    )(wires, flips, gates)


def runs(slots):
    merged = []
    for at, (piece, place) in enumerate(slots):
        if merged and merged[-1][0] == piece and merged[-1][1] + merged[-1][3] == place:
            merged[-1][3] += 1
        else:
            merged.append([piece, place, at, 1])
    return merged


def stack(pieces, axis):
    return pieces[0] if len(pieces) == 1 else jnp.concatenate(pieces, axis=axis)


def left(matrix, loads):
    columns = jnp.concatenate([jnp.concatenate(pair, axis=0) for pair in loads], axis=1)
    out = product((matrix[0], matrix[1]), halves(columns))
    order = matrix.shape[-1] // 2
    return [
        (out[:order, k * order : (k + 1) * order], out[order:, k * order : (k + 1) * order])
        for k in range(len(loads))
    ]


def right(pairs, lane):
    order = lane.shape[-1] // 2
    rows = jnp.concatenate([jnp.concatenate(pair, axis=1) for pair in pairs], axis=0)
    rows = product(halves(rows), (lane[0], lane[1]))
    return [
        (rows[k * order : (k + 1) * order, :order], rows[k * order : (k + 1) * order, order:])
        for k in range(len(pairs))
    ]


def top_gate(matrix, chunk, sources, in_slots, targets, out_slots):
    order = matrix.shape[-1] // 2
    step = 2 * chunk
    per = min(2, chunk)

    def span(height, place, count, m, part):
        return pl.ds(place * height * step + 2 * m + part, count * height, stride=step)

    def body(i, carry):
        ms = [per * i + k for k in range(per)]
        tall = order // len(in_slots)
        loads = [
            tuple(
                stack([sources[o][span(tall, p, n, m, part), :] for o, p, _, n in runs(in_slots)], 0)
                for part in range(2)
            )
            for m in ms
        ]
        tall = order // len(out_slots)
        for m, pair in zip(ms, left(matrix, loads)):
            for part in range(2):
                for o, p, at, n in runs(out_slots):
                    targets[o][span(tall, p, n, m, part), :] = pair[part][at * tall : (at + n) * tall]
        return carry

    lax.fori_loop(0, chunk // per, body, 0)


def top_kernel(chunk, in_slots, out_slots, count, matrix, *refs):
    top_gate(matrix, chunk, refs[:count], in_slots, refs[count:], out_slots)


def final_kernel(chunk, in_slots, count, at, matrix, *refs):
    sources, out, scratch, semaphore = refs[:count], refs[-3], refs[-2], refs[-1]
    top_gate(matrix, chunk, sources, in_slots, [scratch], [(0, 0)])
    order = matrix.shape[-1] // 2
    copy = pltpu.make_async_copy(
        scratch.reshape(order, 2 * chunk, scratch.shape[-1]),
        out.at[:, pl.ds(2 * chunk * at, 2 * chunk), :],
        semaphore,
    )
    copy.start()
    copy.wait()


def inner_kernel(chunk, low, groups, matrix, lane, *refs):
    half = len(refs) // 2
    chunks = half // groups
    rows = low * chunk
    for g in range(groups):
        sources = refs[g * chunks : (g + 1) * chunks]
        targets = refs[half + g * chunks : half + (g + 1) * chunks]
        blocks = sources[0].shape[0] // (2 * rows)
        per = min(2, blocks)

        def body(k, carry, sources=sources, targets=targets, per=per):
            starts = [pl.multiple_of((per * k + q) * 2 * rows, 2 * rows) for q in range(per)]
            loads = [
                tuple(
                    stack([s[pl.ds(start + part, rows, stride=2), :] for s in sources], 0)
                    for part in range(2)
                )
                for start in starts
            ]
            for start, pair in zip(starts, right(left(matrix, loads), lane)):
                for part in range(2):
                    for c, t in enumerate(targets):
                        t[pl.ds(start + part, rows, stride=2), :] = pair[part][c * rows : (c + 1) * rows]
            return carry

        lax.fori_loop(0, blocks // per, body, 0)


def call(kernel, name, mats, sources, out_rows, lanes):
    return [
        keep(out)
        for out in pl.pallas_call(
            kernel,
            out_shape=[pltpu.VMEM((rows, lanes), F32) for rows in out_rows],
            in_specs=[VMEM] * (len(mats) + len(sources)),
            out_specs=[VMEM] * len(out_rows),
            compiler_params=LIMIT,
            name=name,
        )(*mats, *sources)
    ]


def split_by(bit, count):
    slots, filled = [], [0, 0]
    for s in range(count):
        side = s >> bit & 1
        slots.append((side, filled[side]))
        filled[side] += 1
    return slots


def gather_kernel(height, moves, *refs):
    for o, p, at, n in moves:
        refs[-1][pl.ds(at * height, n * height), :] = refs[o][pl.ds(p * height, n * height), :]


def exchange(order, slots, pieces, height):
    slots, pieces = list(slots), list(pieces)
    for step, (axis, bit, slot_bit) in enumerate(order):
        leaving = [s for s in range(len(slots)) if s >> slot_bit & 1]
        if step == 0:
            send = pieces[1]
        else:
            moves = runs([slots[s] for s in leaving])
            used = sorted({o for o, _, _, _ in moves})
            send = pl.pallas_call(
                functools.partial(gather_kernel, height, [(used.index(o), p, at, n) for o, p, at, n in moves]),
                out_shape=pltpu.VMEM((len(leaving) * height, pieces[0].shape[1]), F32),
                in_specs=[VMEM] * len(used),
                out_specs=VMEM,
                compiler_params=LIMIT,
                name="gather",
            )(*[pieces[o] for o in used])
        pairs = [(i, i ^ (1 << bit)) for i in range(lax.axis_size(axis))]
        pieces.append(keep(lax.ppermute(send, axis, pairs)))
        for at, s in enumerate(leaving):
            slots[s] = (len(pieces) - 1, at)
    used = sorted({o for o, _ in slots})
    return [(used.index(o), p) for o, p in slots], [pieces[o] for o in used]


def pack_kernel(chunk, at, slots, own, source, *refs):
    targets, semaphores = refs[:2], refs[2]
    copies = [
        pltpu.make_async_copy(
            source.at[jnp.bitwise_xor(own[0], s), :, pl.ds(2 * chunk * at, 2 * chunk), :],
            targets[o].at[p],
            semaphores.at[s],
        )
        for s, (o, p) in enumerate(slots)
    ]
    for copy in copies:
        copy.start()
    for copy in copies:
        copy.wait()


def pack(own, source, chunk, at, slots):
    count, height, _, lanes = source.shape
    shape = (count // 2, height, 2 * chunk, lanes)
    outs = pl.pallas_call(
        functools.partial(pack_kernel, chunk, at, slots),
        out_shape=[pltpu.VMEM(shape, F32)] * 2,
        in_specs=[SMEM, ANY],
        out_specs=[VMEM] * 2,
        scratch_shapes=[pltpu.SemaphoreType.DMA((count,))],
        compiler_params=LIMIT,
        name="pack",
    )(own, source)
    return [keep(out.reshape(-1, lanes)) for out in outs]


def rotate(order, by):
    by %= len(order)
    return order[by:] + order[:by]


def shards(amplitudes, gates, gate_wires):
    count = amplitudes.shape[1]
    order = gates.shape[-1]
    middle = count // (order * order)
    low = order // middle
    chunk = 4
    chunks = middle // chunk
    top = bits_of(order)
    nx, ny, nz = (bits_of(lax.axis_size(a)) for a in ("gx", "gy", "gz"))
    assert nx < top - bits_of(low)

    at_x, at_z = lax.axis_index("gx"), lax.axis_index("gz")
    at_yz = lax.axis_index("gy") * lax.axis_size("gz") + at_z
    in_1 = jnp.left_shift(at_yz, top - ny - nz)
    by_x = jnp.left_shift(at_x, top - nx)
    by_z = jnp.left_shift(at_z, top - nz)
    zero = jnp.zeros_like(by_x)
    flips = jnp.stack([zero, zero, by_x, in_1, zero, zero, by_z, by_x, zero, zero, zero, by_z])
    lane, m1, m2, m3, m5 = [keep(m) for m in matrices(gates, gate_wires, flips.reshape(6, 2), middle, chunks)]

    slots_1, slots_2, slots_3 = 1 << (ny + nz), 1 << nx, 1 << nz
    links = [("gz", b, b) for b in reversed(range(1, nz))] + [("gy", b, nz + b) for b in range(ny)]
    links = links[-1:] + links[:-1]
    near = [("gz", 0, 0)]
    links_3 = [("gz", b, b) for b in reversed(range(1, nz))]
    links_2 = [("gx", b, b) for b in reversed(range(nx))]

    rows = amplitudes.reshape(2, count // order, order)
    rows = with_layout_constraint(rows, Layout((1, 0, 2)))
    source = rows.transpose(1, 0, 2).reshape(slots_1, order // slots_1, 2 * middle, order)

    def rows_of(share):
        return order * 2 * chunk // share

    packed = []
    for c in range(chunks):
        steps = rotate(links, c) + near
        slots = split_by(steps[0][2], slots_1)
        packed.append((steps, slots, pack(at_yz.reshape(1), source, chunk, c, slots)))
    first = []
    out_slots = []
    for s in range(slots_2):
        side, place = divmod(s, slots_2 // 2)
        out_slots += [(side, place), (2 + side, place)]
    for c in range(chunks):
        steps, slots, pieces = packed[c]
        slots, pieces = exchange(steps, slots, pieces, rows_of(slots_1))
        first.append(
            call(
                functools.partial(top_kernel, chunk, slots, out_slots, len(pieces)),
                "first", (m1,), pieces, [rows_of(4)] * 4, order,
            )
        )

    def cross(stays, leaves):
        slots = [divmod(s, slots_2 // 2) for s in range(slots_2)]
        return exchange(links_2, slots, [stays, leaves], rows_of(2 * slots_2))

    def inner(groups, name):
        flat = [piece for group in groups for piece in group]
        outs = call(
            functools.partial(inner_kernel, chunk, low, len(groups)),
            name, (m2, lane), flat, [piece.shape[0] for piece in flat], order,
        )
        return [outs[g * chunks : (g + 1) * chunks] for g in range(len(groups))]

    early = [cross(p[0], p[1]) for p in first]
    late = inner([[p[2] for p in first], [p[3] for p in first]], "inner_late")
    early_slots = early[0][0]
    moved = inner([[e[1][k] for e in early] for k in range(len(early[0][1]))], "inner_early")
    crossed = [cross(late[0][c], late[1][c]) for c in range(chunks)]

    result = None
    for c in range(chunks):
        pieces = [group[c] for group in moved]
        in_slots = []
        for s in range(slots_2):
            o, p = crossed[c][0][s]
            in_slots += [early_slots[s], (len(pieces) + o, p)]
        pieces = pieces + crossed[c][1]
        steps = rotate(links_3, c) + near
        slots = split_by(steps[0][2], slots_3)
        pieces = call(
            functools.partial(top_kernel, chunk, in_slots, slots, len(pieces)),
            "third", (m3,), pieces, [rows_of(2)] * 2, order,
        )
        slots, pieces = exchange(steps, slots, pieces, rows_of(slots_3))
        extra = [] if result is None else [result]
        result = pl.pallas_call(
            functools.partial(final_kernel, chunk, slots, len(pieces), c),
            out_shape=jax.ShapeDtypeStruct((order, 2 * middle, order), F32),
            in_specs=[VMEM] * (1 + len(pieces)) + [ANY] * len(extra),
            out_specs=ANY,
            scratch_shapes=[pltpu.VMEM((rows_of(1), order), F32), pltpu.SemaphoreType.DMA],
            input_output_aliases={1 + len(pieces): 0} if extra else {},
            compiler_params=LIMIT,
            name="last",
        )(m5, *pieces, *extra)
    return result.reshape(count // order, 2, order).transpose(1, 0, 2).reshape(2, count)


def solution(mesh):
    in_specs = (P(None, ("gx", "gy", "gz")), P(), P())
    out_specs = P(None, ("gx", "gy", "gz"))
    return jax.shard_map(shards, mesh=mesh, in_specs=in_specs, out_specs=out_specs, check_vma=False)
```

time: 155 us -> 116 us (0.75)
  blocking collectives: 31.5 us -> 0 us
  starting transfers between devices: 8.9 us -> 37.5 us
  waiting for transfers between devices: 69.9 us -> 48.3 us
  local copies, waits for them, and re-layouts: 13.4 us -> 3.87 us
  Pallas kernels: 30.4 us -> 26.1 us
    ppermute x1 -> x36, starting transfers between devices: 2.59 us -> 37.5 us  [exchange(): pieces.append(keep(lax.ppermute(send, axis, pairs)))]
    all_to_all x1 -> x0, blocking collectives: 31.5 us -> none  [shards(): lax.all_to_all(state, 'gz', split_axis=0, concat_axis=0, tiled=True)]
    all_to_all x1 -> x0, waiting for transfers between devices: 24.3 us -> none  [shards(): lax.all_to_all(state, ('gy', 'gz'), split_axis=0, concat_axis=0, tiled=True)]
    transpose x1 -> x0, local copies, waits for them, and re-layouts: 8.55 us -> none  [shards(): amplitudes.reshape(2, count // order, order).transpose(1, 0, 2)]
    all_to_all x1 -> x0, starting transfers between devices: 6.32 us -> none  [shards(): lax.all_to_all(state, ('gy', 'gz'), split_axis=0, concat_axis=0, tiled=True)]
    pallas_call x4 -> x39, Pallas kernels: 30.4 us -> 26.1 us  [the longest x10 13.4 us: call(): pl.pallas_call(kernel, out_shape=[pltpu.VMEM((rows, lanes), F32) for rows...]
    ppermute x1 -> x36, waiting for transfers between devices: 45.6 us -> 48.3 us  [exchange(): pieces.append(keep(lax.ppermute(send, axis, pairs)))]
    unnamed x5 -> x18, local copies, waits for them, and re-layouts: 4.08 us -> 3.7 us
  transfers between devices with their start and end apart: 2 -> 36, of which waited for: 2 -> 22; matrix products, arithmetic and copies ran while one was open for 0% -> 0% of each run, Pallas kernels for 3% -> 21%
where the time goes in v1:
time: 116 us
  waiting for transfers between devices  48.3 us (42%)
  starting transfers between devices  37.5 us (32%)
  Pallas kernels  26.1 us (22%)
  local copies, waits for them, and re-layouts  3.87 us (3%)
    ppermute x36, waiting for transfers between devices, exchange(): pieces.append(keep(lax.ppermute(send, axis, pairs)))  48.3 us
    ppermute x36, starting transfers between devices, exchange(): pieces.append(keep(lax.ppermute(send, axis, pairs)))  37.5 us
    pallas_call x10, Pallas kernels, call(): pl.pallas_call(kernel, out_shape=[pltpu.VMEM((rows, lanes), F32) for rows...  13.4 us
    pallas_call x4, Pallas kernels, shards(): pl.pallas_call(functools.partial(final_kernel, chunk, slots, len(pieces),...  5.45 us
    unnamed x18, local copies, waits for them, and re-layouts  3.7 us
    pallas_call x20, Pallas kernels, exchange(): pl.pallas_call(functools.partial(gather_kernel, height, [(used.index(o),...  3.34 us
    pallas_call x1, Pallas kernels, matrices(): pl.pallas_call(functools.partial(matrices_kernel, middle, chunks), out_sh...  2.77 us
  transfers between devices with their start and end apart: 36, of which 22 were waited for; matrix products, arithmetic and copies ran while one was open for 0% of the time, Pallas kernels for 21%

profile of v1, /device:TPU:0, one launch (start us, length us, event | category | flops | bytes accessed | tf_op | source)
XLA Modules:
  0.0 116.2 jit_solution(14002038625323591555)
XLA Ops:
  0.0 1.6 %copy-done = f32[2,262144]{1,0:T(2,128)S(1)} copy-done((f32[2,262144]{1,0:T(2,128)S(1)}, f32[2,262144]{1,0:T(2,128)}, u32[]{:S(2)}) %copy-start) | copy-done | bytes 2097176
  1.9 3.1 %collective-permute-start.12 = (f32[512,128]{1,0:T(8,128)S(1)}, f32[512,128]{1,0:T(8,128)S(1)}, u32[]{:S(2)}, u32[]{:S(2)}) collective-permute-start(f32[512,128]{1,0:T(8,128)S(1)} %bitcast.45), channel_id=1, source_target_pairs={{0,8},{8,0},{1,9},{9,1},{2,10},{10,2},{3,11},{11,3},{4,12},{12,4},... | collective-permute-start | bytes 786440 | tf_op jit(solution)/shard_map/ppermute | solution.py:274
  5.3 1.6 %collective-permute-start.8 = (f32[512,128]{1,0:T(8,128)S(1)}, f32[512,128]{1,0:T(8,128)S(1)}, u32[]{:S(2)}, u32[]{:S(2)}) collective-permute-start(f32[512,128]{1,0:T(8,128)S(1)} %bitcast.44), channel_id=1, source_target_pairs={{0,2},{1,3},{2,0},{3,1},{4,6},{5,7},{6,4},{7,5},{8,10},{9,11},{10,... | collective-permute-start | bytes 786440 | tf_op jit(solution)/shard_map/ppermute | solution.py:274
  7.1 1.6 %collective-permute-start.4 = (f32[512,128]{1,0:T(8,128)S(1)}, f32[512,128]{1,0:T(8,128)S(1)}, u32[]{:S(2)}, u32[]{:S(2)}) collective-permute-start(f32[512,128]{1,0:T(8,128)S(1)} %bitcast.43), channel_id=1, source_target_pairs={{0,4},{1,5},{2,6},{3,7},{4,0},{5,1},{6,2},{7,3},{8,12},{9,13},{10,... | collective-permute-start | bytes 786440 | tf_op jit(solution)/shard_map/ppermute | solution.py:274
  9.5 2.5 %collective-permute-done.12.refs_1_ = f32[512,128]{1,0:T(8,128)S(1)} collective-permute-done((f32[512,128]{1,0:T(8,128)S(1)}, f32[512,128]{1,0:T(8,128)S(1)}, u32[]{:S(2)}, u32[]{:S(2)}) %collective-permute-start.12) | collective-permute-done | bytes 262176 | tf_op jit(solution)/shard_map/ppermute | solution.py:274
  12.0 2.2 %collective-permute-start.13 = (f32[512,128]{1,0:T(8,128)S(1)}, f32[512,128]{1,0:T(8,128)S(1)}, u32[]{:S(2)}, u32[]{:S(2)}) collective-permute-start(f32[512,128]{1,0:T(8,128)S(1)} %gather.29), channel_id=1, source_target_pairs={{0,4},{1,5},{2,6},{3,7},{4,0},{5,1},{6,2},{7,3},{8,12},{9,13},{10,... | collective-permute-start | bytes 786440 | tf_op jit(solution)/shard_map/ppermute | solution.py:274
  14.2 1.6 %collective-permute-start.9 = (f32[512,128]{1,0:T(8,128)S(1)}, f32[512,128]{1,0:T(8,128)S(1)}, u32[]{:S(2)}, u32[]{:S(2)}) collective-permute-start(f32[512,128]{1,0:T(8,128)S(1)} %gather.26), channel_id=1, source_target_pairs={{0,8},{8,0},{1,9},{9,1},{2,10},{10,2},{3,11},{11,3},{4,12},{12,4},... | collective-permute-start | bytes 786440 | tf_op jit(solution)/shard_map/ppermute | solution.py:274
  16.1 1.3 %collective-permute-start.5 = (f32[512,128]{1,0:T(8,128)S(1)}, f32[512,128]{1,0:T(8,128)S(1)}, u32[]{:S(2)}, u32[]{:S(2)}) collective-permute-start(f32[512,128]{1,0:T(8,128)S(1)} %gather.23), channel_id=1, source_target_pairs={{0,2},{1,3},{2,0},{3,1},{4,6},{5,7},{6,4},{7,5},{8,10},{9,11},{10,... | collective-permute-start | bytes 786440 | tf_op jit(solution)/shard_map/ppermute | solution.py:274
  18.2 1.6 %collective-permute-start.1 = (f32[512,128]{1,0:T(8,128)S(1)}, f32[512,128]{1,0:T(8,128)S(1)}, u32[]{:S(2)}, u32[]{:S(2)}) collective-permute-start(f32[512,128]{1,0:T(8,128)S(1)} %gather.20), channel_id=1, source_target_pairs={{0,4},{1,5},{2,6},{3,7},{4,0},{5,1},{6,2},{7,3},{8,12},{9,13},{10,... | collective-permute-start | bytes 786440 | tf_op jit(solution)/shard_map/ppermute | solution.py:274
  19.8 1.9 %collective-permute-done.13.refs_2_ = f32[512,128]{1,0:T(8,128)S(1)} collective-permute-done((f32[512,128]{1,0:T(8,128)S(1)}, f32[512,128]{1,0:T(8,128)S(1)}, u32[]{:S(2)}, u32[]{:S(2)}) %collective-permute-start.13) | collective-permute-done | bytes 262176 | tf_op jit(solution)/shard_map/ppermute | solution.py:274
  22.6 1.7 %collective-permute-start.10 = (f32[512,128]{1,0:T(8,128)S(1)}, f32[512,128]{1,0:T(8,128)S(1)}, u32[]{:S(2)}, u32[]{:S(2)}) collective-permute-start(f32[512,128]{1,0:T(8,128)S(1)} %gather.27), channel_id=1, source_target_pairs={{0,4},{1,5},{2,6},{3,7},{4,0},{5,1},{6,2},{7,3},{8,12},{9,13},{10,... | collective-permute-start | bytes 786440 | tf_op jit(solution)/shard_map/ppermute | solution.py:274
  24.3 1.6 %collective-permute-start.6 = (f32[512,128]{1,0:T(8,128)S(1)}, f32[512,128]{1,0:T(8,128)S(1)}, u32[]{:S(2)}, u32[]{:S(2)}) collective-permute-start(f32[512,128]{1,0:T(8,128)S(1)} %gather.24), channel_id=1, source_target_pairs={{0,8},{8,0},{1,9},{9,1},{2,10},{10,2},{3,11},{11,3},{4,12},{12,4},... | collective-permute-start | bytes 786440 | tf_op jit(solution)/shard_map/ppermute | solution.py:274
  26.0 1.5 %collective-permute-done.1.refs_2_ = f32[512,128]{1,0:T(8,128)S(1)} collective-permute-done((f32[512,128]{1,0:T(8,128)S(1)}, f32[512,128]{1,0:T(8,128)S(1)}, u32[]{:S(2)}, u32[]{:S(2)}) %collective-permute-start.1) | collective-permute-done | bytes 262176 | tf_op jit(solution)/shard_map/ppermute | solution.py:274
  27.6 1.6 %collective-permute-done.14.refs_3_ = f32[512,128]{1,0:T(8,128)S(1)} collective-permute-done((f32[512,128]{1,0:T(8,128)S(1)}, f32[512,128]{1,0:T(8,128)S(1)}, u32[]{:S(2)}, u32[]{:S(2)}) %collective-permute-start.14) | collective-permute-done | bytes 262176 | tf_op jit(solution)/shard_map/ppermute | solution.py:274
  30.0 1.5 %collective-permute-done.10.refs_3_ = f32[512,128]{1,0:T(8,128)S(1)} collective-permute-done((f32[512,128]{1,0:T(8,128)S(1)}, f32[512,128]{1,0:T(8,128)S(1)}, u32[]{:S(2)}, u32[]{:S(2)}) %collective-permute-start.10) | collective-permute-done | bytes 262176 | tf_op jit(solution)/shard_map/ppermute | solution.py:274
  32.3 0.8 gather.25
  34.9 1.1 copy-done.7
  36.0 2.8 %matrices.1 = (bf16[2,256,256]{2,1,0:T(8,128)(2,1)S(1)}, bf16[2,256,256]{2,1,0:T(8,128)(2,1)S(1)}, bf16[2,256,256]{2,1,0:T(8,128)(2,1)S(1)}, bf16[2,256,256]{2,1,0:T(8,128)(2,1)S(1)}, bf16[2,256,256]{2,1,0:T(8,128)(2,1)S(1)}) custom-call(s32[6,7]{1,0:T(8,128)S(1)} %copy-done.8, s32[6,2]{1,0:T(8,128)S(1)} %reshape.45.flips, f32[6,2,128,128]{3,2,1,0:T(8,128)S(1)} %copy-done.7), custom_call_target="tpu_custom_call" | custom-call | tf_op jit(solution)/shard_map/matrices/pallas_call | solution.py:111
  38.8 0.9 copy-done.6
  39.8 1.5 %first.7 = (f32[256,128]{1,0:T(8,128)S(1)}, f32[256,128]{1,0:T(8,128)S(1)}, f32[256,128]{1,0:T(8,128)S(1)}, f32[256,128]{1,0:T(8,128)S(1)}) custom-call(bf16[2,256,256]{2,1,0:T(8,128)(2,1)S(1)} %get-tuple-element.62.matrix, f32[512,128]{1,0:T(8,128)S(1)} %bitcast.41, f32[512,128]{1,0:T(8,128)S(1)} %collective-permute-done.12.refs_1_, ...), custom_call_target="tpu_custom_call" | custom-call | tf_op jit(solution)/shard_map/first/pallas_call | solution.py:231
  41.3 2.6 %collective-permute-start.19 = (f32[256,128]{1,0:T(8,128)S(1)}, f32[256,128]{1,0:T(8,128)S(1)}, u32[]{:S(2)}, u32[]{:S(2)}) collective-permute-start(f32[256,128]{1,0:T(8,128)S(1)} %get-tuple-element.78), channel_id=1, source_target_pairs={{0,16},{16,0},{1,17},{17,1},{2,18},{18,2},{3,19},{19,3},{4,20},{20... | collective-permute-start | bytes 393224 | tf_op jit(solution)/shard_map/ppermute | solution.py:274
  43.9 1.5 %first.6 = (f32[256,128]{1,0:T(8,128)S(1)}, f32[256,128]{1,0:T(8,128)S(1)}, f32[256,128]{1,0:T(8,128)S(1)}, f32[256,128]{1,0:T(8,128)S(1)}) custom-call(bf16[2,256,256]{2,1,0:T(8,128)(2,1)S(1)} %get-tuple-element.62.matrix, f32[512,128]{1,0:T(8,128)S(1)} %bitcast.37, f32[512,128]{1,0:T(8,128)S(1)} %collective-permute-done.8.refs_1_, ...), custom_call_target="tpu_custom_call" | custom-call | tf_op jit(solution)/shard_map/first/pallas_call | solution.py:231
  45.9 1.5 %first.5 = (f32[256,128]{1,0:T(8,128)S(1)}, f32[256,128]{1,0:T(8,128)S(1)}, f32[256,128]{1,0:T(8,128)S(1)}, f32[256,128]{1,0:T(8,128)S(1)}) custom-call(bf16[2,256,256]{2,1,0:T(8,128)(2,1)S(1)} %get-tuple-element.62.matrix, f32[512,128]{1,0:T(8,128)S(1)} %bitcast.33, f32[512,128]{1,0:T(8,128)S(1)} %collective-permute-done.4.refs_1_, ...), custom_call_target="tpu_custom_call" | custom-call | tf_op jit(solution)/shard_map/first/pallas_call | solution.py:231
  47.4 2.6 %collective-permute-start.17 = (f32[256,128]{1,0:T(8,128)S(1)}, f32[256,128]{1,0:T(8,128)S(1)}, u32[]{:S(2)}, u32[]{:S(2)}) collective-permute-start(f32[256,128]{1,0:T(8,128)S(1)} %get-tuple-element.76), channel_id=1, source_target_pairs={{0,16},{16,0},{1,17},{17,1},{2,18},{18,2},{3,19},{19,3},{4,20},{20... | collective-permute-start | bytes 393224 | tf_op jit(solution)/shard_map/ppermute | solution.py:274
  50.0 1.5 %first.4 = (f32[256,128]{1,0:T(8,128)S(1)}, f32[256,128]{1,0:T(8,128)S(1)}, f32[256,128]{1,0:T(8,128)S(1)}, f32[256,128]{1,0:T(8,128)S(1)}) custom-call(bf16[2,256,256]{2,1,0:T(8,128)(2,1)S(1)} %get-tuple-element.62.matrix, f32[512,128]{1,0:T(8,128)S(1)} %bitcast.29, f32[512,128]{1,0:T(8,128)S(1)} %collective-permute-done.refs_1_, ...), custom_call_target="tpu_custom_call" | custom-call | tf_op jit(solution)/shard_map/first/pallas_call | solution.py:231
  52.0 2.6 %inner_late.1 = (f32[256,128]{1,0:T(8,128)S(1)}, f32[256,128]{1,0:T(8,128)S(1)}, f32[256,128]{1,0:T(8,128)S(1)}, f32[256,128]{1,0:T(8,128)S(1)}, f32[256,128]{1,...) custom-call(bf16[2,256,256]{2,1,0:T(8,128)(2,1)S(1)} %get-tuple-element.60.matrix, ...), custom_call_target="tpu_custom_call" | custom-call | tf_op jit(solution)/shard_map/inner_late/pallas_call | solution.py:231
  54.5 2.6 %collective-permute-start.32 = (f32[256,128]{1,0:T(8,128)S(1)}, f32[256,128]{1,0:T(8,128)S(1)}, u32[]{:S(2)}, u32[]{:S(2)}) collective-permute-start(f32[256,128]{1,0:T(8,128)S(1)} %get-tuple-element.108), channel_id=1, source_target_pairs={{0,16},{16,0},{1,17},{17,1},{2,18},{18,2},{3,19},{19,3},{4,20},{20... | collective-permute-start | bytes 393224 | tf_op jit(solution)/shard_map/ppermute | solution.py:274
  57.1 4.6 %collective-permute-done.19.refs_7_ = f32[256,128]{1,0:T(8,128)S(1)} collective-permute-done((f32[256,128]{1,0:T(8,128)S(1)}, f32[256,128]{1,0:T(8,128)S(1)}, u32[]{:S(2)}, u32[]{:S(2)}) %collective-permute-start.19) | collective-permute-done | bytes 131104 | tf_op jit(solution)/shard_map/ppermute | solution.py:274
  61.8 4.2 %collective-permute-done.18.refs_6_ = f32[256,128]{1,0:T(8,128)S(1)} collective-permute-done((f32[256,128]{1,0:T(8,128)S(1)}, f32[256,128]{1,0:T(8,128)S(1)}, u32[]{:S(2)}, u32[]{:S(2)}) %collective-permute-start.18) | collective-permute-done | bytes 131104 | tf_op jit(solution)/shard_map/ppermute | solution.py:274
  66.0 5.6 %collective-permute-done.17.refs_5_ = f32[256,128]{1,0:T(8,128)S(1)} collective-permute-done((f32[256,128]{1,0:T(8,128)S(1)}, f32[256,128]{1,0:T(8,128)S(1)}, u32[]{:S(2)}, u32[]{:S(2)}) %collective-permute-start.17) | collective-permute-done | bytes 131104 | tf_op jit(solution)/shard_map/ppermute | solution.py:274
  71.6 4.2 %collective-permute-done.16.refs_4_ = f32[256,128]{1,0:T(8,128)S(1)} collective-permute-done((f32[256,128]{1,0:T(8,128)S(1)}, f32[256,128]{1,0:T(8,128)S(1)}, u32[]{:S(2)}, u32[]{:S(2)}) %collective-permute-start.16) | collective-permute-done | bytes 131104 | tf_op jit(solution)/shard_map/ppermute | solution.py:274
  75.8 2.6 %inner_early.1 = (f32[256,128]{1,0:T(8,128)S(1)}, f32[256,128]{1,0:T(8,128)S(1)}, f32[256,128]{1,0:T(8,128)S(1)}, f32[256,128]{1,0:T(8,128)S(1)}, f32[256,128]{1...) custom-call(bf16[2,256,256]{2,1,0:T(8,128)(2,1)S(1)} %get-tuple-element.60.matrix, ...), custom_call_target="tpu_custom_call" | custom-call | tf_op jit(solution)/shard_map/inner_early/pallas_call | solution.py:231
  78.4 3.0 %collective-permute-done.32.refs_3_ = f32[256,128]{1,0:T(8,128)S(1)} collective-permute-done((f32[256,128]{1,0:T(8,128)S(1)}, f32[256,128]{1,0:T(8,128)S(1)}, u32[]{:S(2)}, u32[]{:S(2)}) %collective-permute-start.32) | collective-permute-done | bytes 131104 | tf_op jit(solution)/shard_map/ppermute | solution.py:274
  82.1 2.2 %collective-permute-done.28.refs_3_ = f32[256,128]{1,0:T(8,128)S(1)} collective-permute-done((f32[256,128]{1,0:T(8,128)S(1)}, f32[256,128]{1,0:T(8,128)S(1)}, u32[]{:S(2)}, u32[]{:S(2)}) %collective-permute-start.28) | collective-permute-done | bytes 131104 | tf_op jit(solution)/shard_map/ppermute | solution.py:274
  84.8 1.5 %collective-permute-start.29 = (f32[512,128]{1,0:T(8,128)S(1)}, f32[512,128]{1,0:T(8,128)S(1)}, u32[]{:S(2)}, u32[]{:S(2)}) collective-permute-start(f32[512,128]{1,0:T(8,128)S(1)} %get-tuple-element.104), channel_id=1, source_target_pairs={{0,2},{1,3},{2,0},{3,1},{4,6},{5,7},{6,4},{7,5},{8,10},{9,11},{10,... | collective-permute-start | bytes 786440 | tf_op jit(solution)/shard_map/ppermute | solution.py:274
  87.6 1.6 %collective-permute-start.25 = (f32[512,128]{1,0:T(8,128)S(1)}, f32[512,128]{1,0:T(8,128)S(1)}, u32[]{:S(2)}, u32[]{:S(2)}) collective-permute-start(f32[512,128]{1,0:T(8,128)S(1)} %get-tuple-element.98), channel_id=1, source_target_pairs={{0,4},{1,5},{2,6},{3,7},{4,0},{5,1},{6,2},{7,3},{8,12},{9,13},{10,... | collective-permute-start | bytes 786440 | tf_op jit(solution)/shard_map/ppermute | solution.py:274
  90.4 1.5 %collective-permute-start.21 = (f32[512,128]{1,0:T(8,128)S(1)}, f32[512,128]{1,0:T(8,128)S(1)}, u32[]{:S(2)}, u32[]{:S(2)}) collective-permute-start(f32[512,128]{1,0:T(8,128)S(1)} %get-tuple-element.92), channel_id=1, source_target_pairs={{0,2},{1,3},{2,0},{3,1},{4,6},{5,7},{6,4},{7,5},{8,10},{9,11},{10,... | collective-permute-start | bytes 786440 | tf_op jit(solution)/shard_map/ppermute | solution.py:274
  93.1 1.6 %collective-permute-start.30 = (f32[512,128]{1,0:T(8,128)S(1)}, f32[512,128]{1,0:T(8,128)S(1)}, u32[]{:S(2)}, u32[]{:S(2)}) collective-permute-start(f32[512,128]{1,0:T(8,128)S(1)} %gather.36), channel_id=1, source_target_pairs={{0,4},{1,5},{2,6},{3,7},{4,0},{5,1},{6,2},{7,3},{8,12},{9,13},{10,... | collective-permute-start | bytes 786440 | tf_op jit(solution)/shard_map/ppermute | solution.py:274
  94.7 2.1 %collective-permute-done.25.refs_1_ = f32[512,128]{1,0:T(8,128)S(1)} collective-permute-done((f32[512,128]{1,0:T(8,128)S(1)}, f32[512,128]{1,0:T(8,128)S(1)}, u32[]{:S(2)}, u32[]{:S(2)}) %collective-permute-start.25) | collective-permute-done | bytes 262176 | tf_op jit(solution)/shard_map/ppermute | solution.py:274
  96.9 1.5 %collective-permute-start.26 = (f32[512,128]{1,0:T(8,128)S(1)}, f32[512,128]{1,0:T(8,128)S(1)}, u32[]{:S(2)}, u32[]{:S(2)}) collective-permute-start(f32[512,128]{1,0:T(8,128)S(1)} %gather.34), channel_id=1, source_target_pairs={{0,2},{1,3},{2,0},{3,1},{4,6},{5,7},{6,4},{7,5},{8,10},{9,11},{10,... | collective-permute-start | bytes 786440 | tf_op jit(solution)/shard_map/ppermute | solution.py:274
  98.4 1.2 %collective-permute-done.21.refs_1_ = f32[512,128]{1,0:T(8,128)S(1)} collective-permute-done((f32[512,128]{1,0:T(8,128)S(1)}, f32[512,128]{1,0:T(8,128)S(1)}, u32[]{:S(2)}, u32[]{:S(2)}) %collective-permute-start.21) | collective-permute-done | bytes 262176 | tf_op jit(solution)/shard_map/ppermute | solution.py:274
  99.6 1.6 %collective-permute-start.22 = (f32[512,128]{1,0:T(8,128)S(1)}, f32[512,128]{1,0:T(8,128)S(1)}, u32[]{:S(2)}, u32[]{:S(2)}) collective-permute-start(f32[512,128]{1,0:T(8,128)S(1)} %gather.32), channel_id=1, source_target_pairs={{0,4},{1,5},{2,6},{3,7},{4,0},{5,1},{6,2},{7,3},{8,12},{9,13},{10,... | collective-permute-start | bytes 786440 | tf_op jit(solution)/shard_map/ppermute | solution.py:274
  101.2 4.0 %collective-permute-done.34.refs_2_ = f32[512,128]{1,0:T(8,128)S(1)} collective-permute-done((f32[512,128]{1,0:T(8,128)S(1)}, f32[512,128]{1,0:T(8,128)S(1)}, u32[]{:S(2)}, u32[]{:S(2)}) %collective-permute-start.34) | collective-permute-done | bytes 262176 | tf_op jit(solution)/shard_map/ppermute | solution.py:274
  105.9 4.0 %collective-permute-done.26.refs_2_ = f32[512,128]{1,0:T(8,128)S(1)} collective-permute-done((f32[512,128]{1,0:T(8,128)S(1)}, f32[512,128]{1,0:T(8,128)S(1)}, u32[]{:S(2)}, u32[]{:S(2)}) %collective-permute-start.26) | collective-permute-done | bytes 262176 | tf_op jit(solution)/shard_map/ppermute | solution.py:274
  110.6 1.4 %last.4.refs_4_ = f32[128,32,128]{2,1,0:T(8,128)} custom-call(bf16[2,256,256]{2,1,0:T(8,128)(2,1)S(1)} %get-tuple-element.58.matrix, f32[512,128]{1,0:T(8,128)S(1)} %get-tuple-element.109.refs_0_, f32[512,128]{1,0:T(8,128)S(1)} %collective-permute-done.33.refs_1_, f32[512,128]{1,0:T(8,128)S(1)} %collective-permute-done.34.refs_2_, ...), custom_call_target="tpu_custom_call" | custom-call | tf_op jit(solution)/shard_map/last/pallas_call | solution.py:405
  112.0 1.4 %last.5.refs_4_ = f32[128,32,128]{2,1,0:T(8,128)} custom-call(bf16[2,256,256]{2,1,0:T(8,128)(2,1)S(1)} %get-tuple-element.58.matrix, f32[512,128]{1,0:T(8,128)S(1)} %get-tuple-element.103.refs_0_, f32[512,128]{1,0:T(8,128)S(1)} %collective-permute-done.29.refs_1_, f32[512,128]{1,0:T(8,128)S(1)} %collective-permute-done.30.refs_2_, ...), custom_call_target="tpu_custom_call", output_to_operand_aliasing={{}: (5, {})} | custom-call | tf_op jit(solution)/shard_map/last/pallas_call | solution.py:405
  113.4 1.4 %last.6.refs_4_ = f32[128,32,128]{2,1,0:T(8,128)} custom-call(bf16[2,256,256]{2,1,0:T(8,128)(2,1)S(1)} %get-tuple-element.58.matrix, f32[512,128]{1,0:T(8,128)S(1)} %get-tuple-element.97.refs_0_, f32[512,128]{1,0:T(8,128)S(1)} %collective-permute-done.25.refs_1_, f32[512,128]{1,0:T(8,128)S(1)} %collective-permute-done.26.refs_2_, ...), custom_call_target="tpu_custom_call", output_to_operand_aliasing={{}: (5, {})} | custom-call | tf_op jit(solution)/shard_map/last/pallas_call | solution.py:405
  114.8 1.4 %last.7 = f32[128,32,128]{2,1,0:T(8,128)} custom-call(bf16[2,256,256]{2,1,0:T(8,128)(2,1)S(1)} %get-tuple-element.58.matrix, f32[512,128]{1,0:T(8,128)S(1)} %get-tuple-element.91.refs_0_, f32[512,128]{1,0:T(8,128)S(1)} %collective-permute-done.21.refs_1_, f32[512,128]{1,0:T(8,128)S(1)} %collective-permute-done.22.refs_2_, ...), custom_call_target="tpu_custom_call", output_to_operand_aliasing={{}: (5, {})} | custom-call | tf_op jit(solution)/shard_map/last/pallas_call | solution.py:405
  (84 shorter events, 14.1 us)
Async XLA Ops:
  0.0 1.6 %copy-start = (f32[2,262144]{1,0:T(2,128)S(1)}, f32[2,262144]{1,0:T(2,128)}, u32[]{:S(2)}) copy-start(f32[2,262144]{1,0:T(2,128)} %param.3) | copy-start | bytes 6291460
  1.9 10.1 %collective-permute-start.12 = (f32[512,128]{1,0:T(8,128)S(1)}, f32[512,128]{1,0:T(8,128)S(1)}, u32[]{:S(2)}, u32[]{:S(2)}) collective-permute-start(f32[512,128]{1,0:T(8,128)S(1)} %bitcast.45), channel_id=1, source_target_pairs={{0,8},{8,0},{1,9},{9,1},{2,10},{10,2},{3,11},{11,3},{4,12},{12,4},... | collective-permute-start | bytes 786440 | tf_op jit(solution)/shard_map/ppermute | solution.py:274
  5.3 8.9 %collective-permute-start.8 = (f32[512,128]{1,0:T(8,128)S(1)}, f32[512,128]{1,0:T(8,128)S(1)}, u32[]{:S(2)}, u32[]{:S(2)}) collective-permute-start(f32[512,128]{1,0:T(8,128)S(1)} %bitcast.44), channel_id=1, source_target_pairs={{0,2},{1,3},{2,0},{3,1},{4,6},{5,7},{6,4},{7,5},{8,10},{9,11},{10,... | collective-permute-start | bytes 786440 | tf_op jit(solution)/shard_map/ppermute | solution.py:274
  7.1 9.0 %collective-permute-start.4 = (f32[512,128]{1,0:T(8,128)S(1)}, f32[512,128]{1,0:T(8,128)S(1)}, u32[]{:S(2)}, u32[]{:S(2)}) collective-permute-start(f32[512,128]{1,0:T(8,128)S(1)} %bitcast.43), channel_id=1, source_target_pairs={{0,4},{1,5},{2,6},{3,7},{4,0},{5,1},{6,2},{7,3},{8,12},{9,13},{10,... | collective-permute-start | bytes 786440 | tf_op jit(solution)/shard_map/ppermute | solution.py:274
  9.0 9.2 %collective-permute-start = (f32[512,128]{1,0:T(8,128)S(1)}, f32[512,128]{1,0:T(8,128)S(1)}, u32[]{:S(2)}, u32[]{:S(2)}) collective-permute-start(f32[512,128]{1,0:T(8,128)S(1)} %bitcast.42), channel_id=1, source_target_pairs={{0,8},{8,0},{1,9},{9,1},{2,10},{10,2},{3,11},{11,3},{4,12},{12,4},... | collective-permute-start | bytes 786440 | tf_op jit(solution)/shard_map/ppermute | solution.py:274
  12.0 9.7 %collective-permute-start.13 = (f32[512,128]{1,0:T(8,128)S(1)}, f32[512,128]{1,0:T(8,128)S(1)}, u32[]{:S(2)}, u32[]{:S(2)}) collective-permute-start(f32[512,128]{1,0:T(8,128)S(1)} %gather.29), channel_id=1, source_target_pairs={{0,4},{1,5},{2,6},{3,7},{4,0},{5,1},{6,2},{7,3},{8,12},{9,13},{10,... | collective-permute-start | bytes 786440 | tf_op jit(solution)/shard_map/ppermute | solution.py:274
  14.2 8.3 %collective-permute-start.9 = (f32[512,128]{1,0:T(8,128)S(1)}, f32[512,128]{1,0:T(8,128)S(1)}, u32[]{:S(2)}, u32[]{:S(2)}) collective-permute-start(f32[512,128]{1,0:T(8,128)S(1)} %gather.26), channel_id=1, source_target_pairs={{0,8},{8,0},{1,9},{9,1},{2,10},{10,2},{3,11},{11,3},{4,12},{12,4},... | collective-permute-start | bytes 786440 | tf_op jit(solution)/shard_map/ppermute | solution.py:274
  16.1 8.2 %collective-permute-start.5 = (f32[512,128]{1,0:T(8,128)S(1)}, f32[512,128]{1,0:T(8,128)S(1)}, u32[]{:S(2)}, u32[]{:S(2)}) collective-permute-start(f32[512,128]{1,0:T(8,128)S(1)} %gather.23), channel_id=1, source_target_pairs={{0,2},{1,3},{2,0},{3,1},{4,6},{5,7},{6,4},{7,5},{8,10},{9,11},{10,... | collective-permute-start | bytes 786440 | tf_op jit(solution)/shard_map/ppermute | solution.py:274
  18.2 9.2 %collective-permute-start.1 = (f32[512,128]{1,0:T(8,128)S(1)}, f32[512,128]{1,0:T(8,128)S(1)}, u32[]{:S(2)}, u32[]{:S(2)}) collective-permute-start(f32[512,128]{1,0:T(8,128)S(1)} %gather.20), channel_id=1, source_target_pairs={{0,4},{1,5},{2,6},{3,7},{4,0},{5,1},{6,2},{7,3},{8,12},{9,13},{10,... | collective-permute-start | bytes 786440 | tf_op jit(solution)/shard_map/ppermute | solution.py:274
  21.7 7.5 %collective-permute-start.14 = (f32[512,128]{1,0:T(8,128)S(1)}, f32[512,128]{1,0:T(8,128)S(1)}, u32[]{:S(2)}, u32[]{:S(2)}) collective-permute-start(f32[512,128]{1,0:T(8,128)S(1)} %gather.30), channel_id=1, source_target_pairs={{0,2},{1,3},{2,0},{3,1},{4,6},{5,7},{6,4},{7,5},{8,10},{9,11},{10,... | collective-permute-start | bytes 786440 | tf_op jit(solution)/shard_map/ppermute | solution.py:274
  22.6 9.0 %collective-permute-start.10 = (f32[512,128]{1,0:T(8,128)S(1)}, f32[512,128]{1,0:T(8,128)S(1)}, u32[]{:S(2)}, u32[]{:S(2)}) collective-permute-start(f32[512,128]{1,0:T(8,128)S(1)} %gather.27), channel_id=1, source_target_pairs={{0,4},{1,5},{2,6},{3,7},{4,0},{5,1},{6,2},{7,3},{8,12},{9,13},{10,... | collective-permute-start | bytes 786440 | tf_op jit(solution)/shard_map/ppermute | solution.py:274
  24.3 8.0 %collective-permute-start.6 = (f32[512,128]{1,0:T(8,128)S(1)}, f32[512,128]{1,0:T(8,128)S(1)}, u32[]{:S(2)}, u32[]{:S(2)}) collective-permute-start(f32[512,128]{1,0:T(8,128)S(1)} %gather.24), channel_id=1, source_target_pairs={{0,8},{8,0},{1,9},{9,1},{2,10},{10,2},{3,11},{11,3},{4,12},{12,4},... | collective-permute-start | bytes 786440 | tf_op jit(solution)/shard_map/ppermute | solution.py:274
  27.5 6.4 %collective-permute-start.2 = (f32[512,128]{1,0:T(8,128)S(1)}, f32[512,128]{1,0:T(8,128)S(1)}, u32[]{:S(2)}, u32[]{:S(2)}) collective-permute-start(f32[512,128]{1,0:T(8,128)S(1)} %gather.21), channel_id=1, source_target_pairs={{0,2},{1,3},{2,0},{3,1},{4,6},{5,7},{6,4},{7,5},{8,10},{9,11},{10,... | collective-permute-start | bytes 786440 | tf_op jit(solution)/shard_map/ppermute | solution.py:274
  29.2 5.5 %copy-start.5 = (f32[512,128]{1,0:T(8,128)}, f32[512,128]{1,0:T(8,128)S(1)}, u32[]{:S(2)}) copy-start(f32[512,128]{1,0:T(8,128)S(1)} %collective-permute-done.14.refs_3_) | copy-start | bytes 786436
  30.0 4.9 %copy-start.8 = (s32[6,7]{1,0:T(8,128)S(1)}, s32[6,7]{1,0:T(8,128)}, u32[]{:S(2)}) copy-start(s32[6,7]{1,0:T(8,128)} %wires.1) | copy-start | bytes 508
  30.0 8.8 %collective-permute-start.15 = (f32[512,128]{1,0:T(8,128)}, f32[512,128]{1,0:T(8,128)}, u32[]{:S(2)}, u32[]{:S(2)}) collective-permute-start(f32[512,128]{1,0:T(8,128)} %gather.31), channel_id=1, source_target_pairs={{0,1},{1,0},{2,3},{3,2},{4,5},{5,4},{6,7},{7,6},{8,9},{9,8},{10,11... | collective-permute-start | bytes 786440 | tf_op jit(solution)/shard_map/ppermute | solution.py:274
  31.5 3.2 %copy-start.3 = (f32[512,128]{1,0:T(8,128)}, f32[512,128]{1,0:T(8,128)S(1)}, u32[]{:S(2)}) copy-start(f32[512,128]{1,0:T(8,128)S(1)} %collective-permute-done.10.refs_3_) | copy-start | bytes 786436
  32.3 11.6 %collective-permute-start.11 = (f32[512,128]{1,0:T(8,128)}, f32[512,128]{1,0:T(8,128)}, u32[]{:S(2)}, u32[]{:S(2)}) collective-permute-start(f32[512,128]{1,0:T(8,128)} %gather.28), channel_id=1, source_target_pairs={{0,1},{1,0},{2,3},{3,2},{4,5},{5,4},{6,7},{7,6},{8,9},{9,8},{10,11... | collective-permute-start | bytes 786440 | tf_op jit(solution)/shard_map/ppermute | solution.py:274
  32.3 1.7 %copy-start.1 = (f32[512,128]{1,0:T(8,128)}, f32[512,128]{1,0:T(8,128)S(1)}, u32[]{:S(2)}) copy-start(f32[512,128]{1,0:T(8,128)S(1)} %collective-permute-done.6.refs_3_) | copy-start | bytes 786436
  33.1 12.8 %collective-permute-start.7 = (f32[512,128]{1,0:T(8,128)}, f32[512,128]{1,0:T(8,128)}, u32[]{:S(2)}, u32[]{:S(2)}) collective-permute-start(f32[512,128]{1,0:T(8,128)} %gather.25), channel_id=1, source_target_pairs={{0,1},{1,0},{2,3},{3,2},{4,5},{5,4},{6,7},{7,6},{8,9},{9,8},{10,11... | collective-permute-start | bytes 786440 | tf_op jit(solution)/shard_map/ppermute | solution.py:274
  34.7 15.3 %collective-permute-start.3 = (f32[512,128]{1,0:T(8,128)}, f32[512,128]{1,0:T(8,128)}, u32[]{:S(2)}, u32[]{:S(2)}) collective-permute-start(f32[512,128]{1,0:T(8,128)} %gather.22), channel_id=1, source_target_pairs={{0,1},{1,0},{2,3},{3,2},{4,5},{5,4},{6,7},{7,6},{8,9},{9,8},{10,11... | collective-permute-start | bytes 786440 | tf_op jit(solution)/shard_map/ppermute | solution.py:274
  34.9 1.1 copy-start.7
  36.0 7.9 %copy-start.4 = (f32[512,128]{1,0:T(8,128)S(1)}, f32[512,128]{1,0:T(8,128)}, u32[]{:S(2)}) copy-start(f32[512,128]{1,0:T(8,128)} %copy-done.3) | copy-start | bytes 786436
  36.0 9.8 %copy-start.2 = (f32[512,128]{1,0:T(8,128)S(1)}, f32[512,128]{1,0:T(8,128)}, u32[]{:S(2)}) copy-start(f32[512,128]{1,0:T(8,128)} %copy-done.1) | copy-start | bytes 786436
  38.8 1.0 copy-start.6
  41.3 20.5 %collective-permute-start.19 = (f32[256,128]{1,0:T(8,128)S(1)}, f32[256,128]{1,0:T(8,128)S(1)}, u32[]{:S(2)}, u32[]{:S(2)}) collective-permute-start(f32[256,128]{1,0:T(8,128)S(1)} %get-tuple-element.78), channel_id=1, source_target_pairs={{0,16},{16,0},{1,17},{17,1},{2,18},{18,2},{3,19},{19,3},{4,20},{20... | collective-permute-start | bytes 393224 | tf_op jit(solution)/shard_map/ppermute | solution.py:274
  45.4 20.6 %collective-permute-start.18 = (f32[256,128]{1,0:T(8,128)S(1)}, f32[256,128]{1,0:T(8,128)S(1)}, u32[]{:S(2)}, u32[]{:S(2)}) collective-permute-start(f32[256,128]{1,0:T(8,128)S(1)} %get-tuple-element.77), channel_id=1, source_target_pairs={{0,16},{16,0},{1,17},{17,1},{2,18},{18,2},{3,19},{19,3},{4,20},{20... | collective-permute-start | bytes 393224 | tf_op jit(solution)/shard_map/ppermute | solution.py:274
  47.4 24.2 %collective-permute-start.17 = (f32[256,128]{1,0:T(8,128)S(1)}, f32[256,128]{1,0:T(8,128)S(1)}, u32[]{:S(2)}, u32[]{:S(2)}) collective-permute-start(f32[256,128]{1,0:T(8,128)S(1)} %get-tuple-element.76), channel_id=1, source_target_pairs={{0,16},{16,0},{1,17},{17,1},{2,18},{18,2},{3,19},{19,3},{4,20},{20... | collective-permute-start | bytes 393224 | tf_op jit(solution)/shard_map/ppermute | solution.py:274
  51.5 24.3 %collective-permute-start.16 = (f32[256,128]{1,0:T(8,128)S(1)}, f32[256,128]{1,0:T(8,128)S(1)}, u32[]{:S(2)}, u32[]{:S(2)}) collective-permute-start(f32[256,128]{1,0:T(8,128)S(1)} %get-tuple-element.75), channel_id=1, source_target_pairs={{0,16},{16,0},{1,17},{17,1},{2,18},{18,2},{3,19},{19,3},{4,20},{20... | collective-permute-start | bytes 393224 | tf_op jit(solution)/shard_map/ppermute | solution.py:274
  54.5 26.9 %collective-permute-start.32 = (f32[256,128]{1,0:T(8,128)S(1)}, f32[256,128]{1,0:T(8,128)S(1)}, u32[]{:S(2)}, u32[]{:S(2)}) collective-permute-start(f32[256,128]{1,0:T(8,128)S(1)} %get-tuple-element.108), channel_id=1, source_target_pairs={{0,16},{16,0},{1,17},{17,1},{2,18},{18,2},{3,19},{19,3},{4,20},{20... | collective-permute-start | bytes 393224 | tf_op jit(solution)/shard_map/ppermute | solution.py:274
  61.8 22.5 %collective-permute-start.28 = (f32[256,128]{1,0:T(8,128)S(1)}, f32[256,128]{1,0:T(8,128)S(1)}, u32[]{:S(2)}, u32[]{:S(2)}) collective-permute-start(f32[256,128]{1,0:T(8,128)S(1)} %get-tuple-element.102), channel_id=1, source_target_pairs={{0,16},{16,0},{1,17},{17,1},{2,18},{18,2},{3,19},{19,3},{4,20},{20... | collective-permute-start | bytes 393224 | tf_op jit(solution)/shard_map/ppermute | solution.py:274
  66.0 21.1 %collective-permute-start.24 = (f32[256,128]{1,0:T(8,128)S(1)}, f32[256,128]{1,0:T(8,128)S(1)}, u32[]{:S(2)}, u32[]{:S(2)}) collective-permute-start(f32[256,128]{1,0:T(8,128)S(1)} %get-tuple-element.96), channel_id=1, source_target_pairs={{0,16},{16,0},{1,17},{17,1},{2,18},{18,2},{3,19},{19,3},{4,20},{20... | collective-permute-start | bytes 393224 | tf_op jit(solution)/shard_map/ppermute | solution.py:274
  71.6 18.2 %collective-permute-start.20 = (f32[256,128]{1,0:T(8,128)S(1)}, f32[256,128]{1,0:T(8,128)S(1)}, u32[]{:S(2)}, u32[]{:S(2)}) collective-permute-start(f32[256,128]{1,0:T(8,128)S(1)} %get-tuple-element.90), channel_id=1, source_target_pairs={{0,16},{16,0},{1,17},{17,1},{2,18},{18,2},{3,19},{19,3},{4,20},{20... | collective-permute-start | bytes 393224 | tf_op jit(solution)/shard_map/ppermute | solution.py:274
  82.0 9.9 %collective-permute-start.33 = (f32[512,128]{1,0:T(8,128)S(1)}, f32[512,128]{1,0:T(8,128)S(1)}, u32[]{:S(2)}, u32[]{:S(2)}) collective-permute-start(f32[512,128]{1,0:T(8,128)S(1)} %get-tuple-element.110), channel_id=1, source_target_pairs={{0,4},{1,5},{2,6},{3,7},{4,0},{5,1},{6,2},{7,3},{8,12},{9,13},{10,... | collective-permute-start | bytes 786440 | tf_op jit(solution)/shard_map/ppermute | solution.py:274
  84.8 8.3 %collective-permute-start.29 = (f32[512,128]{1,0:T(8,128)S(1)}, f32[512,128]{1,0:T(8,128)S(1)}, u32[]{:S(2)}, u32[]{:S(2)}) collective-permute-start(f32[512,128]{1,0:T(8,128)S(1)} %get-tuple-element.104), channel_id=1, source_target_pairs={{0,2},{1,3},{2,0},{3,1},{4,6},{5,7},{6,4},{7,5},{8,10},{9,11},{10,... | collective-permute-start | bytes 786440 | tf_op jit(solution)/shard_map/ppermute | solution.py:274
  87.6 9.2 %collective-permute-start.25 = (f32[512,128]{1,0:T(8,128)S(1)}, f32[512,128]{1,0:T(8,128)S(1)}, u32[]{:S(2)}, u32[]{:S(2)}) collective-permute-start(f32[512,128]{1,0:T(8,128)S(1)} %get-tuple-element.98), channel_id=1, source_target_pairs={{0,4},{1,5},{2,6},{3,7},{4,0},{5,1},{6,2},{7,3},{8,12},{9,13},{10,... | collective-permute-start | bytes 786440 | tf_op jit(solution)/shard_map/ppermute | solution.py:274
  90.4 9.2 %collective-permute-start.21 = (f32[512,128]{1,0:T(8,128)S(1)}, f32[512,128]{1,0:T(8,128)S(1)}, u32[]{:S(2)}, u32[]{:S(2)}) collective-permute-start(f32[512,128]{1,0:T(8,128)S(1)} %get-tuple-element.92), channel_id=1, source_target_pairs={{0,2},{1,3},{2,0},{3,1},{4,6},{5,7},{6,4},{7,5},{8,10},{9,11},{10,... | collective-permute-start | bytes 786440 | tf_op jit(solution)/shard_map/ppermute | solution.py:274
  91.9 13.3 %collective-permute-start.34 = (f32[512,128]{1,0:T(8,128)S(1)}, f32[512,128]{1,0:T(8,128)S(1)}, u32[]{:S(2)}, u32[]{:S(2)}) collective-permute-start(f32[512,128]{1,0:T(8,128)S(1)} %gather.38), channel_id=1, source_target_pairs={{0,2},{1,3},{2,0},{3,1},{4,6},{5,7},{6,4},{7,5},{8,10},{9,11},{10,... | collective-permute-start | bytes 786440 | tf_op jit(solution)/shard_map/ppermute | solution.py:274
  93.1 12.2 %collective-permute-start.30 = (f32[512,128]{1,0:T(8,128)S(1)}, f32[512,128]{1,0:T(8,128)S(1)}, u32[]{:S(2)}, u32[]{:S(2)}) collective-permute-start(f32[512,128]{1,0:T(8,128)S(1)} %gather.36), channel_id=1, source_target_pairs={{0,4},{1,5},{2,6},{3,7},{4,0},{5,1},{6,2},{7,3},{8,12},{9,13},{10,... | collective-permute-start | bytes 786440 | tf_op jit(solution)/shard_map/ppermute | solution.py:274
  96.9 13.1 %collective-permute-start.26 = (f32[512,128]{1,0:T(8,128)S(1)}, f32[512,128]{1,0:T(8,128)S(1)}, u32[]{:S(2)}, u32[]{:S(2)}) collective-permute-start(f32[512,128]{1,0:T(8,128)S(1)} %gather.34), channel_id=1, source_target_pairs={{0,2},{1,3},{2,0},{3,1},{4,6},{5,7},{6,4},{7,5},{8,10},{9,11},{10,... | collective-permute-start | bytes 786440 | tf_op jit(solution)/shard_map/ppermute | solution.py:274
  99.6 10.4 %collective-permute-start.22 = (f32[512,128]{1,0:T(8,128)S(1)}, f32[512,128]{1,0:T(8,128)S(1)}, u32[]{:S(2)}, u32[]{:S(2)}) collective-permute-start(f32[512,128]{1,0:T(8,128)S(1)} %gather.32), channel_id=1, source_target_pairs={{0,4},{1,5},{2,6},{3,7},{4,0},{5,1},{6,2},{7,3},{8,12},{9,13},{10,... | collective-permute-start | bytes 786440 | tf_op jit(solution)/shard_map/ppermute | solution.py:274
  105.3 5.4 %collective-permute-start.35 = (f32[512,128]{1,0:T(8,128)S(1)}, f32[512,128]{1,0:T(8,128)S(1)}, u32[]{:S(2)}, u32[]{:S(2)}) collective-permute-start(f32[512,128]{1,0:T(8,128)S(1)} %gather.39), channel_id=1, source_target_pairs={{0,1},{1,0},{2,3},{3,2},{4,5},{5,4},{6,7},{7,6},{8,9},{9,8},{10,11... | collective-permute-start | bytes 786440 | tf_op jit(solution)/shard_map/ppermute | solution.py:274
  105.4 6.6 %collective-permute-start.31 = (f32[512,128]{1,0:T(8,128)S(1)}, f32[512,128]{1,0:T(8,128)S(1)}, u32[]{:S(2)}, u32[]{:S(2)}) collective-permute-start(f32[512,128]{1,0:T(8,128)S(1)} %gather.37), channel_id=1, source_target_pairs={{0,1},{1,0},{2,3},{3,2},{4,5},{5,4},{6,7},{7,6},{8,9},{9,8},{10,11... | collective-permute-start | bytes 786440 | tf_op jit(solution)/shard_map/ppermute | solution.py:274
  110.0 3.4 %collective-permute-start.27 = (f32[512,128]{1,0:T(8,128)S(1)}, f32[512,128]{1,0:T(8,128)S(1)}, u32[]{:S(2)}, u32[]{:S(2)}) collective-permute-start(f32[512,128]{1,0:T(8,128)S(1)} %gather.35), channel_id=1, source_target_pairs={{0,1},{1,0},{2,3},{3,2},{4,5},{5,4},{6,7},{7,6},{8,9},{9,8},{10,11... | collective-permute-start | bytes 786440 | tf_op jit(solution)/shard_map/ppermute | solution.py:274
  110.1 4.7 %collective-permute-start.23 = (f32[512,128]{1,0:T(8,128)S(1)}, f32[512,128]{1,0:T(8,128)S(1)}, u32[]{:S(2)}, u32[]{:S(2)}) collective-permute-start(f32[512,128]{1,0:T(8,128)S(1)} %gather.33), channel_id=1, source_target_pairs={{0,1},{1,0},{2,3},{3,2},{4,5},{5,4},{6,7},{7,6},{8,9},{9,8},{10,11... | collective-permute-start | bytes 786440 | tf_op jit(solution)/shard_map/ppermute | solution.py:274
